TPU v7x, 32 devices: a whole 2x2x4 slice. The times are simulated.
32 devices in a mesh: seq: 8 (over z, y), dp: 4 (over x, core).
Axes of the slice: x: 2, y: 2, z: 4, core: 2. Of those that a mesh axis runs over, the one named last changes fastest.
Arguments:
- block_input: bfloat16 [4, 1024, 1536], P('dp', 'seq'), may hold values from -6 to 6
- query_proj: bfloat16 [4, 1024, 768], P('dp', 'seq'), may hold values from -8 to 8
- key_proj: bfloat16 [4, 1024, 768], P('dp', 'seq'), may hold values from -8 to 8
- value_proj: bfloat16 [4, 1024, 768], P('dp', 'seq'), may hold values from -6 to 6
- lengths: int32 [4], P('dp'), may hold values from 256 to 1024, as said below
- out_proj: bfloat16 [1536, 768], replicated, may hold values from -0.21875 to 0.21875
- kernel: float32 [31, 1536], replicated, may hold values from -1 to 1
- conv_bias: float32 [1536], replicated, may hold values from -3 to 3
- grad_output: bfloat16 [4, 1024, 1536], P('dp', 'seq'), may hold values from -6 to 6
Outputs:
- block_output: bfloat16 [4, 1024, 1536], P('dp', 'seq')
- grad_input: bfloat16 [4, 1024, 1536], P('dp', 'seq')
- grad_query: bfloat16 [4, 1024, 768], P('dp', 'seq')
- grad_out_proj: float32 [1536, 768], P('seq')
- grad_kernel: float32 [31, 1536], P(None, 'seq')
- grad_bias: float32 [1536], P('seq')
Inputs may be any that keep to these rules, and one draw needn't show every extreme that they name: `lengths`: frames at or after an utterance's length are padding; in every draw at least one utterance has all 1024 frames valid.
All inputs are finite; a program needn't handle non-finite values.
Results may differ from a plain program's by a relative error of at most 0.012.
The roundings to bfloat16 on the way count: a program that leaves them out, or rounds other values in their place, can miss the bound.
Values may be sent and summed in bfloat16 or wider, within the bound.
No kernel may reach another device: no remote copies, remote signals or barrier semaphores. Data moves between devices by JAX's collectives and lax.ppermute only.
A program may use at most 128 MiB of HBM per device.

v0:
```python
import math
import jax
import jax.numpy as jnp
from jax import lax
from jax.sharding import PartitionSpec as P

D = 1536
H = 8
HS = 96
KW = 31
HD = 768


def with_halo(x, sides, width):
    for axis, dim in sides:
        size, length = (lax.axis_size(axis), x.shape[dim])
        up = [(i, (i + 1) % size) for i in range(size - 1)]
        down = [(j, i) for i, j in up]
        last = lax.slice_in_dim(x, length - width, length, axis=dim)
        leading = lax.slice_in_dim(x, 0, width, axis=dim)
        before = lax.ppermute(last, axis, up)
        after = lax.ppermute(leading, axis, down)
        x = jnp.concatenate([before, x, after], axis=dim)
    return x


def forward_rows(query_one, key_one, value_one, key_valid, score_scale):
    row_total = query_one.shape[0]
    block_rows = math.gcd(row_total, 512)
    query_blocks = query_one.reshape(row_total // block_rows, block_rows, query_one.shape[1])

    def forward_one_block(query_block):
        scores = (
            lax.dot_general(
                query_block, key_one, (((1,), (1,)), ((), ())), preferred_element_type=jnp.float32
            )
            * score_scale
        )
        scores = jnp.where(key_valid[None, :], scores, -jnp.inf)
        row_top = jnp.max(scores, axis=-1, keepdims=True)
        log_total = row_top + jnp.log(jnp.sum(jnp.exp(scores - row_top), axis=-1, keepdims=True))
        weights = jnp.exp(scores - log_total).astype(jnp.bfloat16)
        return (jnp.dot(weights, value_one, preferred_element_type=jnp.float32), log_total[:, 0])

    outputs, log_totals = lax.map(forward_one_block, query_blocks)
    return (outputs.reshape(row_total, query_one.shape[1]), log_totals.reshape(row_total))


def backward_rows(
    query_one, key_one, value_one, grad_one, lse_one, delta_one, key_valid, score_scale
):
    row_total = query_one.shape[0]
    block_rows = math.gcd(row_total, 512)
    block_count = row_total // block_rows
    width = query_one.shape[1]

    def backward_one_block(items):
        query_block, grad_block, lse_block, delta_block = items
        scores = (
            lax.dot_general(
                query_block, key_one, (((1,), (1,)), ((), ())), preferred_element_type=jnp.float32
            )
            * score_scale
        )
        scores = jnp.where(key_valid[None, :], scores, -jnp.inf)
        probs = jnp.exp(scores - lse_block[:, None])
        grad_prob = lax.dot_general(
            grad_block, value_one, (((1,), (1,)), ((), ())), preferred_element_type=jnp.float32
        )
        grad_score = (probs * (grad_prob - delta_block[:, None])).astype(jnp.bfloat16)
        return jnp.dot(grad_score, key_one, preferred_element_type=jnp.float32) * score_scale

    results = lax.map(
        backward_one_block,
        (
            query_one.reshape(block_count, block_rows, width),
            grad_one.reshape(block_count, block_rows, width),
            lse_one.reshape(block_count, block_rows),
            delta_one.reshape(block_count, block_rows),
        ),
    )
    return results.reshape(row_total, width)


def on_device(
    block_input, query_proj, key_proj, value_proj, lengths, out_proj, kernel, conv_bias, grad_output
):
    frames_dev = block_input.shape[1]
    seq_count = lax.axis_size("seq")
    total_frames = frames_dev * seq_count
    first_frame = lax.axis_index("seq") * frames_dev
    utt_length = lengths[0]
    local_valid = first_frame + jnp.arange(frames_dev) < utt_length
    all_valid = jnp.arange(total_frames) < utt_length
    score_scale = 1.0 / math.sqrt(HS)
    halo_width = KW // 2
    group_size = seq_count // H
    sub_rows = frames_dev // group_size
    query_local = query_proj[0]

    def to_serving(matrix):
        return matrix.reshape(frames_dev, H, HS).transpose(1, 0, 2).reshape(seq_count, sub_rows, HS)

    def from_serving(returned):
        return returned.reshape(H, frames_dev, HS).transpose(1, 0, 2).reshape(frames_dev, HD)

    query_mine = lax.all_to_all(
        to_serving(query_local), "seq", split_axis=0, concat_axis=1, tiled=True
    )[0]
    key_send = jnp.repeat(
        key_proj[0].reshape(frames_dev, H, HS).transpose(1, 0, 2), group_size, axis=0
    )
    value_send = jnp.repeat(
        value_proj[0].reshape(frames_dev, H, HS).transpose(1, 0, 2), group_size, axis=0
    )
    key_mine, value_mine = (
        lax.all_to_all(key_send, "seq", split_axis=0, concat_axis=1, tiled=True),
        lax.all_to_all(value_send, "seq", split_axis=0, concat_axis=1, tiled=True),
    )
    key_mine = key_mine[0]
    value_mine = value_mine[0]
    head_out, head_lse = forward_rows(query_mine, key_mine, value_mine, all_valid, score_scale)
    head_attended = head_out.astype(jnp.bfloat16)
    attended = from_serving(
        lax.all_to_all(head_attended[None], "seq", split_axis=1, concat_axis=0, tiled=True)
    )
    projected = lax.dot_general(
        attended, out_proj, (((1,), (1,)), ((), ())), preferred_element_type=jnp.float32
    )
    mixed_rows = (block_input[0].astype(jnp.float32) + projected).astype(jnp.bfloat16)
    masked = jnp.where(local_valid[:, None], mixed_rows, jnp.zeros_like(mixed_rows))
    padded = with_halo(masked, (("seq", 0),), halo_width).astype(jnp.float32)
    conv_rows = jnp.broadcast_to(conv_bias, (frames_dev, D))
    for tap in range(KW):
        conv_rows = conv_rows + kernel[tap] * padded[tap : tap + frames_dev]
    gate_rows = jax.nn.sigmoid(conv_rows)
    block_output = jnp.where(
        local_valid[:, None], mixed_rows.astype(jnp.float32) + conv_rows * gate_rows, 0.0
    ).astype(jnp.bfloat16)
    grad_rows = jnp.where(local_valid[:, None], grad_output[0].astype(jnp.float32), 0.0)
    grad_conv = grad_rows * gate_rows * (1.0 + conv_rows * (1.0 - gate_rows))
    kernel_local = jnp.stack(
        [jnp.sum(grad_conv * padded[tap : tap + frames_dev], axis=0) for tap in range(KW)]
    )
    bias_local = jnp.sum(grad_conv, axis=0)
    grad_padded = with_halo(grad_conv, (("seq", 0),), halo_width)
    grad_masked = jnp.zeros((frames_dev, D), jnp.float32)
    for tap in range(KW):
        begin = 2 * halo_width - tap
        grad_masked = grad_masked + kernel[tap] * grad_padded[begin : begin + frames_dev]
    grad_input = (grad_rows + jnp.where(local_valid[:, None], grad_masked, 0.0)).astype(
        jnp.bfloat16
    )
    grad_attn = jnp.dot(grad_input, out_proj, preferred_element_type=jnp.float32).astype(
        jnp.bfloat16
    )
    grad_mine = lax.all_to_all(
        to_serving(grad_attn), "seq", split_axis=0, concat_axis=1, tiled=True
    )[0]
    delta_mine = jnp.sum(grad_mine.astype(jnp.float32) * head_attended.astype(jnp.float32), axis=-1)
    grad_q_mine = backward_rows(
        query_mine, key_mine, value_mine, grad_mine, head_lse, delta_mine, all_valid, score_scale
    ).astype(jnp.bfloat16)
    grad_query = from_serving(
        lax.all_to_all(grad_q_mine[None], "seq", split_axis=1, concat_axis=0, tiled=True)
    )
    term_block = lax.dot_general(
        grad_input, attended, (((0,), (0,)), ((), ())), preferred_element_type=jnp.float32
    )
    partial_rows = lax.psum_scatter(term_block, "seq", scatter_dimension=0, tiled=True)
    summed = lax.psum(partial_rows.astype(jnp.bfloat16), "dp").astype(jnp.float32)
    kernel_total, bias_total = lax.psum((kernel_local, bias_local), ("seq", "dp"))
    shard_width = D // seq_count
    offset = lax.axis_index("seq") * shard_width
    grad_kernel = lax.dynamic_slice_in_dim(kernel_total, offset, shard_width, 1)
    grad_bias = lax.dynamic_slice_in_dim(bias_total, offset, shard_width, 0)
    return (block_output[None], grad_input[None], grad_query[None], summed, grad_kernel, grad_bias)


def solution(mesh):
    placed = (
        P("dp", "seq", None),
        P("dp", "seq", None),
        P("dp", "seq", None),
        P("dp", "seq", None),
        P("dp"),
        P(),
        P(),
        P(),
        P("dp", "seq", None),
    )
    return jax.shard_map(
        on_device,
        mesh=mesh,
        in_specs=placed,
        out_specs=(
            P("dp", "seq", None),
            P("dp", "seq", None),
            P("dp", "seq", None),
            P("seq", None),
            P(None, "seq"),
            P("seq"),
        ),
        check_vma=False,
    )
```

profile of v0, /device:TPU:0, one launch (start us, length us, event | category | flops | bytes accessed | tf_op | source)
XLA Modules:
  0.0 321.5 jit_solution(12944451114000263372)
XLA Ops:
  9.9 7.3 %all-to-all-start = ((bf16[8,128,96]{1,2,0:T(8,128)(2,1)}), bf16[8,128,96]{1,2,0:T(8,128)(2,1)S(1)}, u32[]{:S(2)}, u32[]{:S(2)}) async-start(bf16[8,128,96]{1,2,0:T(8,128)(2,1)} %bitcast.3), calls=%async_computation | async-start | bytes 393216 | tf_op jit(solution)/shard_map/all_to_all | solution.py:107
  18.9 6.2 %all-to-all-done = bf16[8,128,96]{1,2,0:T(8,128)(2,1)S(1)} async-done(((bf16[8,128,96]{1,2,0:T(8,128)(2,1)}), bf16[8,128,96]{1,2,0:T(8,128)(2,1)S(1)}, u32[]{:S(2)}, u32[]{:S(2)}) %all-to-all-start) | async-done | bytes 196640 | tf_op jit(solution)/shard_map/all_to_all | solution.py:107
  25.1 3.4 %all-to-all-start.1 = ((bf16[8,128,96]{1,2,0:T(8,128)(2,1)}), bf16[8,128,96]{1,2,0:T(8,128)(2,1)S(1)}, u32[]{:S(2)}, u32[]{:S(2)}) async-start(bf16[8,128,96]{1,2,0:T(8,128)(2,1)} %bitcast.5), calls=%async_computation.1 | async-start | bytes 393216 | tf_op jit(solution)/shard_map/all_to_all | solution.py:117
  30.3 6.0 %all-to-all-done.1 = bf16[8,128,96]{1,2,0:T(8,128)(2,1)S(1)} async-done(((bf16[8,128,96]{1,2,0:T(8,128)(2,1)}), bf16[8,128,96]{1,2,0:T(8,128)(2,1)S(1)}, u32[]{:S(2)}, u32[]{:S(2)}) %all-to-all-start.1) | async-done | bytes 196640 | tf_op jit(solution)/shard_map/all_to_all | solution.py:117
  36.3 3.4 %all-to-all-start.2 = ((bf16[8,128,96]{1,2,0:T(8,128)(2,1)}), bf16[8,128,96]{1,2,0:T(8,128)(2,1)S(1)}, u32[]{:S(2)}, u32[]{:S(2)}) async-start(bf16[8,128,96]{1,2,0:T(8,128)(2,1)} %bitcast.7), calls=%async_computation.2 | async-start | bytes 393216 | tf_op jit(solution)/shard_map/all_to_all | solution.py:118
  40.0 7.3 %all-to-all-done.2 = bf16[8,128,96]{1,2,0:T(8,128)(2,1)S(1)} async-done(((bf16[8,128,96]{1,2,0:T(8,128)(2,1)}), bf16[8,128,96]{1,2,0:T(8,128)(2,1)S(1)}, u32[]{:S(2)}, u32[]{:S(2)}) %all-to-all-start.2) | async-done | bytes 196640 | tf_op jit(solution)/shard_map/all_to_all | solution.py:118
  47.6 4.6 %while.24 = (s32[]{:T(128)}, bf16[2,512,96]{1,2,0:T(8,128)(2,1)S(1)}, f32[2,512]{1,0:T(2,128)S(1)}, bf16[2,512,96]{2,1,0:T(8,128)(2,1)S(1)}, bf16[1024,96]{1,0:T...) while((s32[]{:T(128)}, ...), condition=%wide.region_3.4_spmd.clone, body=%wide.region_0.3_spmd.clone.sunk | while | flops 204997120 | bytes 7164021 | solution.py:45
  56.3 3.7 %reduce.63 = bf16[1024,96]{1,0:T(8,128)(2,1)} reduce(bf16[1024,1,96]{2,1,0:T(2,128)(2,1)} %bitcast.115, bf16[]{:T(256)} %broadcast.73), dimensions={1}, to_apply=%bitcast.66.reduce_sub_computation | reduce | bytes 393218
  62.1 3.4 %all-to-all-start.3 = ((bf16[8,2,6144]{2,1,0:T(2,128)(2,1)}), bf16[8,2,6144]{2,1,0:T(2,128)(2,1)S(1)}, u32[]{:S(2)}, u32[]{:S(2)}) async-start(bf16[8,2,6144]{2,1,0:T(2,128)(2,1)} %reshape.155), calls=%async_computation.3 | async-start | bytes 393216 | tf_op jit(solution)/shard_map/all_to_all | solution.py:125
  69.3 3.9 %all-to-all-done.3 = bf16[8,2,6144]{2,1,0:T(2,128)(2,1)S(1)} async-done(((bf16[8,2,6144]{2,1,0:T(2,128)(2,1)}), bf16[8,2,6144]{2,1,0:T(2,128)(2,1)S(1)}, u32[]{:S(2)}, u32[]{:S(2)}) %all-to-all-start.3) | async-done | bytes 196640 | tf_op jit(solution)/shard_map/all_to_all | solution.py:125
  86.9 7.5 %multiply_reduce_fusion = (f32[1536]{0:T(1024)}, f32[1536]{0:T(1024)}, f32[1536]{0:T(1024)}, f32[1536]{0:T(1024)}, f32[1536]{0:T(1024)}, /*index=5*/f32[1536]{0:...) fusion(f32[158,1536]{1,0:T(8,128)S(1)} %maximum_convert_fusion,, ...), kind=kLoop, calls=%fused_computation.190 | loop fusion | flops 21206016 | bytes 26652800 | tf_op jit(solution)/shard_map/reduce_sum | solution.py:143
  95.7 5.0 %collective-permute-start.3 = (f32[15,1536]{1,0:T(8,128)S(1)}, f32[15,1536]{1,0:T(8,128)S(1)}, u32[]{:S(2)}, u32[]{:S(2)}) collective-permute-start(f32[15,1536]{1,0:T(8,128)S(1)} %get-tuple-element.306), channel_id=1, source_target_pairs={{0,4},{4,8},{8,12},{12,16},{16,20},{20,24},{24,28},{1,5},{5,9},{9,... | collective-permute-start | bytes 276488 | tf_op jit(solution)/shard_map/ppermute | solution.py:21
  102.7 3.7 %fusion.37 = bf16[128,1536]{1,0:T(8,128)(2,1)S(1)} fusion(f32[128,1536]{1,0:T(8,128)S(1)} %get-tuple-element.299, f32[15,1536]{1,0:T(8,128)S(1)} %collective-permute-done.3, f32[15,1536]{1,0:T(8,128)S(1)} %collective-permute-done.2, bf16[1,128,1536]{2,1,0:T(8,128)(2,1)S(1)} %copy-done.11, f32[1536]{0:T(1024)S(1)} %get-tuple-element.265, ...), kind=kLoop, calls=%fused_computation.100 | loop fusion | flops 18874368 | bytes 1947776 | tf_op jit(solution)/shard_map/convert_element_type | solution.py:151
  115.5 6.7 %all-to-all-start.4 = ((bf16[8,128,96]{1,2,0:T(8,128)(2,1)}), bf16[8,128,96]{1,2,0:T(8,128)(2,1)S(1)}, u32[]{:S(2)}, u32[]{:S(2)}) async-start(bf16[8,128,96]{1,2,0:T(8,128)(2,1)} %bitcast.121), calls=%async_computation.4 | async-start | bytes 393216 | tf_op jit(solution)/shard_map/all_to_all | solution.py:157
  128.9 3.5 %stack.127 = f32[31,1536]{1,0:T(8,128)} concatenate(f32[1,1536]{1,0:T(1,128)} %stack.96, f32[1,1536]{1,0:T(1,128)} %stack.97, f32[1,1536]{1,0:T(1,128)} %stack.98, f32[1,1536]{1,0:T(1,128)} %stack.99, f32[1,1536]{1,0:T(1,128)} %stack.100, f32[1,1536]{1,0:T(1,128)S(1)} %stack.101, f32[1,1536]{1,0:T(1,128)S(1)} %stack.102, f32[1,1536]{1,0:T(1,128)S(1)} %stack.103, ...), dimensions={0} | concatenate | bytes 380928 | tf_op jit(solution)/shard_map/stack | solution.py:142
  136.5 12.9 %while.25 = (s32[]{:T(128)}, bf16[2,512,96]{1,2,0:T(8,128)(2,1)}, bf16[2,512,96]{2,1,0:T(8,128)(2,1)S(1)}, bf16[1024,96]{1,0:T(8,128)(2,1)S(1)}, f32[2,512]{1,0:...) while((s32[]{:T(128)}, bf16[2,512,96]{1,2,0:T(8,128)(2,1)}, ...), condition=%wide.region_6.7_spmd.clone, body=%wide.region_5.6_spmd.clone.sunk | while | flops 305185792 | bytes 6241429 | solution.py:73
  139.8 3.3 %fusion.163 = bf16[2,512,96]{1,2,0:T(8,128)(2,1)} fusion(bf16[2,512,96]{1,2,0:T(8,128)(2,1)} %get-tuple-element.455, s32[]{:T(128)S(6)} %copy.133, bf16[1024,96]{1,0:T(8,128)(2,1)S(1)} %get-tuple-element.467, f32[512,1024]{1,0:T(8,128)} %fusion.162, bf16[1024,96]{1,0:T(8,128)(2,1)S(1)} %get-tuple-element.470, f32[512]{0:T(512)S(1)} %bitcast.129, ...), kind=kOutput, calls=%fused_computation.17.clone.1 | convolution fusion | flops 204521472 | bytes 2955264 | tf_op jit(solution)/shard_map/while/body/eval_jaxpr/dot_general | solution.py:71
  146.2 3.2 fusion.163
  154.0 3.7 %reduce.64 = bf16[1024,96]{1,0:T(8,128)(2,1)} reduce(bf16[1024,1,96]{2,1,0:T(2,128)(2,1)} %bitcast.116, bf16[]{:T(256)} %broadcast.73), dimensions={1}, to_apply=%bitcast.68.reduce_sub_computation | reduce | bytes 393218
  159.8 4.5 %all-to-all-start.5 = ((bf16[8,2,6144]{2,1,0:T(2,128)(2,1)}), bf16[8,2,6144]{2,1,0:T(2,128)(2,1)}, u32[]{:S(2)}, u32[]{:S(2)}) async-start(bf16[8,2,6144]{2,1,0:T(2,128)(2,1)} %reshape.157), calls=%async_computation.5 | async-start | bytes 393216 | tf_op jit(solution)/shard_map/all_to_all | solution.py:165
  164.3 48.2 %reduce-scatter.2.cloned.1.call-done = f32[192,768]{1,0:T(8,128)} async-done(((f32[1536,768]{1,0:T(8,128)}), f32[192,768]{1,0:T(8,128)}) %reduce-scatter.2.cloned.1.call-update) | async-done | bytes 589840 | tf_op jit(solution)/shard_map/reduce_scatter | solution.py:170
  215.4 40.3 %psum.23 = f32[1536]{0:T(1024)S(1)} all-reduce(f32[1536]{0:T(1024)S(1)} %copy-done.48), channel_id=1, replica_groups=mesh['seq'=8,'dp'=4] {'seq','dp'}, use_global_device_ids=true, to_apply=%region_42.43 | all-reduce | flops 1536 | bytes 12288 | tf_op jit(solution)/shard_map/psum | solution.py:172
  256.4 20.2 %all-reduce.5.cloned.1.call-done = f32[31,1536]{1,0:T(8,128)} async-done(((f32[31,1536]{1,0:T(8,128)}), f32[31,1536]{1,0:T(8,128)}) %all-reduce.5.cloned.1.call-update) | async-done | bytes 190480 | tf_op jit(solution)/shard_map/psum | solution.py:172
  280.6 31.7 %all-reduce.3.cloned.1.call-done = bf16[192,768]{1,0:T(8,128)(2,1)} async-done(((bf16[192,768]{1,0:T(8,128)(2,1)}), bf16[192,768]{1,0:T(8,128)(2,1)}) %all-reduce.3.cloned.1.call-update) | async-done | bytes 294928 | tf_op jit(solution)/shard_map/psum | solution.py:171
  (218 shorter events, 78.0 us)
Async XLA Ops:
  8.0 67.7 %copy-start = (bf16[1536,768]{1,0:T(8,128)(2,1)S(1)}, bf16[1536,768]{1,0:T(8,128)(2,1)}, u32[]{:S(2)}) copy-start(bf16[1536,768]{1,0:T(8,128)(2,1)} %param.18) | copy-start | bytes 7077892
  9.9 15.2 %all-to-all-start = ((bf16[8,128,96]{1,2,0:T(8,128)(2,1)}), bf16[8,128,96]{1,2,0:T(8,128)(2,1)S(1)}, u32[]{:S(2)}, u32[]{:S(2)}) async-start(bf16[8,128,96]{1,2,0:T(8,128)(2,1)} %bitcast.3), calls=%async_computation | async-start | bytes 393216 | tf_op jit(solution)/shard_map/all_to_all | solution.py:107
  25.1 11.1 %all-to-all-start.1 = ((bf16[8,128,96]{1,2,0:T(8,128)(2,1)}), bf16[8,128,96]{1,2,0:T(8,128)(2,1)S(1)}, u32[]{:S(2)}, u32[]{:S(2)}) async-start(bf16[8,128,96]{1,2,0:T(8,128)(2,1)} %bitcast.5), calls=%async_computation.1 | async-start | bytes 393216 | tf_op jit(solution)/shard_map/all_to_all | solution.py:117
  36.3 11.1 %all-to-all-start.2 = ((bf16[8,128,96]{1,2,0:T(8,128)(2,1)}), bf16[8,128,96]{1,2,0:T(8,128)(2,1)S(1)}, u32[]{:S(2)}, u32[]{:S(2)}) async-start(bf16[8,128,96]{1,2,0:T(8,128)(2,1)} %bitcast.7), calls=%async_computation.2 | async-start | bytes 393216 | tf_op jit(solution)/shard_map/all_to_all | solution.py:118
  52.2 14.0 %copy-start.49 = (f32[2,512]{1,0:T(2,128)}, f32[2,512]{1,0:T(2,128)S(1)}, u32[]{:S(2)}) copy-start(f32[2,512]{1,0:T(2,128)S(1)} %get-tuple-element.448) | copy-start | bytes 12292
  52.3 23.3 %copy-start.1 = (bf16[1024,96]{1,0:T(8,128)(2,1)}, bf16[1024,96]{1,0:T(8,128)(2,1)S(1)}, u32[]{:S(2)}) copy-start(bf16[1024,96]{1,0:T(8,128)(2,1)S(1)} %get-tuple-element.477) | copy-start | bytes 589828
  52.3 23.3 %copy-start.3 = (bf16[1024,96]{1,0:T(8,128)(2,1)}, bf16[1024,96]{1,0:T(8,128)(2,1)S(1)}, u32[]{:S(2)}) copy-start(bf16[1024,96]{1,0:T(8,128)(2,1)S(1)} %get-tuple-element.480) | copy-start | bytes 589828
  52.3 23.3 %copy-start.5 = (bf16[2,512,96]{2,1,0:T(8,128)(2,1)}, bf16[2,512,96]{2,1,0:T(8,128)(2,1)S(1)}, u32[]{:S(2)}) copy-start(bf16[2,512,96]{2,1,0:T(8,128)(2,1)S(1)} %get-tuple-element.481) | copy-start | bytes 589828
  62.1 11.1 %all-to-all-start.3 = ((bf16[8,2,6144]{2,1,0:T(2,128)(2,1)}), bf16[8,2,6144]{2,1,0:T(2,128)(2,1)S(1)}, u32[]{:S(2)}, u32[]{:S(2)}) async-start(bf16[8,2,6144]{2,1,0:T(2,128)(2,1)} %reshape.155), calls=%async_computation.3 | async-start | bytes 393216 | tf_op jit(solution)/shard_map/all_to_all | solution.py:125
  65.5 147.0 %reduce-scatter.2.cloned.1.call-start = ((), (), s32[]{:S(2)}) async-start(), calls=%async_computation.7 | async-start | bytes 5308416 | tf_op jit(solution)/shard_map/reduce_scatter | solution.py:170
  78.6 4.9 %collective-permute-start = (bf16[15,1536]{1,0:T(8,128)(2,1)S(1)}, bf16[15,1536]{1,0:T(8,128)(2,1)S(1)}, u32[]{:S(2)}, u32[]{:S(2)}) collective-permute-start(bf16[15,1536]{1,0:T(8,128)(2,1)S(1)} %get-tuple-element.307), channel_id=1, source_target_pairs={{0,4},{4,8},{8,12},{12,16},{16,20},{20,24},{24,28},{1,5},{5,9},{9,... | collective-permute-start | bytes 138248 | tf_op jit(solution)/shard_map/ppermute | solution.py:21
  80.6 6.0 %collective-permute-start.1 = (bf16[15,1536]{1,0:T(8,128)(2,1)S(1)}, bf16[15,1536]{1,0:T(8,128)(2,1)S(1)}, u32[]{:S(2)}, u32[]{:S(2)}) collective-permute-start(bf16[15,1536]{1,0:T(8,128)(2,1)S(1)} %get-tuple-element.308), channel_id=1, source_target_pairs={{4,0},{8,4},{12,8},{16,12},{20,16},{24,20},{28,24},{5,1},{9,5},{13... | collective-permute-start | bytes 138248 | tf_op jit(solution)/shard_map/ppermute | solution.py:22
  94.4 6.7 %collective-permute-start.2 = (f32[15,1536]{1,0:T(8,128)S(1)}, f32[15,1536]{1,0:T(8,128)S(1)}, u32[]{:S(2)}, u32[]{:S(2)}) collective-permute-start(f32[15,1536]{1,0:T(8,128)S(1)} %get-tuple-element.305), channel_id=1, source_target_pairs={{4,0},{8,4},{12,8},{16,12},{20,16},{24,20},{28,24},{5,1},{9,5},{13... | collective-permute-start | bytes 276488 | tf_op jit(solution)/shard_map/ppermute | solution.py:22
  95.7 7.0 %collective-permute-start.3 = (f32[15,1536]{1,0:T(8,128)S(1)}, f32[15,1536]{1,0:T(8,128)S(1)}, u32[]{:S(2)}, u32[]{:S(2)}) collective-permute-start(f32[15,1536]{1,0:T(8,128)S(1)} %get-tuple-element.306), channel_id=1, source_target_pairs={{0,4},{4,8},{8,12},{12,16},{16,20},{20,24},{24,28},{1,5},{5,9},{9,... | collective-permute-start | bytes 276488 | tf_op jit(solution)/shard_map/ppermute | solution.py:21
  115.5 18.4 %all-to-all-start.4 = ((bf16[8,128,96]{1,2,0:T(8,128)(2,1)}), bf16[8,128,96]{1,2,0:T(8,128)(2,1)S(1)}, u32[]{:S(2)}, u32[]{:S(2)}) async-start(bf16[8,128,96]{1,2,0:T(8,128)(2,1)} %bitcast.121), calls=%async_computation.4 | async-start | bytes 393216 | tf_op jit(solution)/shard_map/all_to_all | solution.py:157
  122.2 154.4 %all-reduce.5.cloned.1.call-start = ((), (), s32[]{:S(2)}) async-start(), calls=%async_computation.9 | async-start | bytes 393216 | tf_op jit(solution)/shard_map/psum | solution.py:172
  125.4 11.2 %copy-start.4 = (bf16[1024,96]{1,0:T(8,128)(2,1)S(1)}, bf16[1024,96]{1,0:T(8,128)(2,1)}, u32[]{:S(2)}) copy-start(bf16[1024,96]{1,0:T(8,128)(2,1)} %copy-done.3) | copy-start | bytes 589828
  125.4 11.2 %copy-start.6 = (bf16[2,512,96]{2,1,0:T(8,128)(2,1)S(1)}, bf16[2,512,96]{2,1,0:T(8,128)(2,1)}, u32[]{:S(2)}) copy-start(bf16[2,512,96]{2,1,0:T(8,128)(2,1)} %copy-done.5) | copy-start | bytes 589828
  149.4 64.9 %copy-start.9 = (f32[128,1536]{1,0:T(8,128)S(1)}, f32[128,1536]{1,0:T(8,128)}, u32[]{:S(2)}) copy-start(f32[128,1536]{1,0:T(8,128)} %get-tuple-element.300) | copy-start | bytes 2359300
  149.5 64.9 %copy-start.10 = (bf16[128,1536]{1,0:T(8,128)(2,1)S(1)}, bf16[128,1536]{1,0:T(8,128)(2,1)}, u32[]{:S(2)}) copy-start(bf16[128,1536]{1,0:T(8,128)(2,1)} %get-tuple-element.310) | copy-start | bytes 1179652
  149.5 64.9 %copy-start.51 = (pred[128]{0:T(512)(128)(4,1)S(1)}, pred[128]{0:T(512)(128)(4,1)}, u32[]{:S(2)}) copy-start(pred[128]{0:T(512)(128)(4,1)} %add_compare_fusion) | copy-start | bytes 388
  154.0 61.4 %copy-start.48 = (f32[1536]{0:T(1024)S(1)}, f32[1536]{0:T(1024)}, u32[]{:S(2)}) copy-start(f32[1536]{0:T(1024)} %get-tuple-element.235) | copy-start | bytes 18436
  159.8 118.3 %all-to-all-start.5 = ((bf16[8,2,6144]{2,1,0:T(2,128)(2,1)}), bf16[8,2,6144]{2,1,0:T(2,128)(2,1)}, u32[]{:S(2)}, u32[]{:S(2)}) async-start(bf16[8,2,6144]{2,1,0:T(2,128)(2,1)} %reshape.157), calls=%async_computation.5 | async-start | bytes 393216 | tf_op jit(solution)/shard_map/all_to_all | solution.py:165
  164.2 148.0 %all-reduce.3.cloned.1.call-start = ((), (), s32[]{:S(2)}) async-start(), calls=%async_computation.8 | async-start | bytes 589824 | tf_op jit(solution)/shard_map/psum | solution.py:171
  (43 other events, 307.3 us)
Sparse Core Ops, SparseCore 0:
  110.3 102.1 reduce-scatter.1
Sparse Core Ops, SparseCore 1:
  132.5 144.0 all-reduce.4
  279.3 32.9 all-reduce.2
where the time goes:
time: 324 us; the launch traced here: 322 us
  waiting for transfers between devices  130 us (40%)
  local copies, waits for them, and re-layouts  44.2 us (14%)
  blocking collectives  40.3 us (12%)
  starting transfers between devices  38.2 us (12%)
  other arithmetic  31.9 us (10%)
  matrix products  19.4 us (6%)
  between operations  17.3 us (5%)
    reduce_scatter x1, waiting for transfers between devices, on_device(): lax.psum_scatter(term_block, 'seq', scatter_dimension=0, tiled=True)  48.2 us
    psum x1, blocking collectives, on_device(): lax.psum((kernel_local, bias_local), ('seq', 'dp'))  40.3 us
    psum x1, waiting for transfers between devices, on_device(): lax.psum(partial_rows.astype(jnp.bfloat16), 'dp').astype(jnp.float32)  31.7 us
    psum x1, waiting for transfers between devices, on_device(): lax.psum((kernel_local, bias_local), ('seq', 'dp'))  20.2 us
    unnamed x119, local copies, waits for them, and re-layouts  15.6 us
    reduce_sum x2, other arithmetic, on_device(): jnp.sum(grad_conv * padded[tap:tap + frames_dev], axis=0)  10.5 us
    unnamed x2, other arithmetic  7.45 us
    all_to_all x1, waiting for transfers between devices, on_device(): lax.all_to_all(value_send, 'seq', split_axis=0, concat_axis=1, tiled=True)  7.34 us
  transfers between devices with their start and end apart: 13, of which 11 were waited for; matrix products, arithmetic and copies ran while one was open for 18% of the time, Pallas kernels for 0%

commit v1 on v0

--- a/solution.py
+++ b/solution.py
@@ -168,7 +168,7 @@
         grad_input, attended, (((0,), (0,)), ((), ())), preferred_element_type=jnp.float32
     )
     partial_rows = lax.psum_scatter(term_block, "seq", scatter_dimension=0, tiled=True)
-    summed = lax.psum(partial_rows.astype(jnp.bfloat16), "dp").astype(jnp.float32)
+    summed = lax.all_gather(partial_rows.astype(jnp.bfloat16), "dp").sum(axis=0).astype(jnp.float32)
     kernel_total, bias_total = lax.psum((kernel_local, bias_local), ("seq", "dp"))
     shard_width = D // seq_count
     offset = lax.axis_index("seq") * shard_width

time: 324 us -> 300 us (0.926)
  waiting for transfers between devices: 130 us -> 106 us
    psum x1 -> x0, waiting for transfers between devices: 31.7 us -> none  [on_device(): lax.psum(partial_rows.astype(jnp.bfloat16), 'dp').astype(jnp.float32)]
    reduce_scatter x1, waiting for transfers between devices: 48.2 us -> 75.6 us  [on_device(): lax.psum_scatter(term_block, 'seq', scatter_dimension=0, tiled=True)]
    psum x1, waiting for transfers between devices: 20.2 us -> 0.01 us  [on_device(): lax.psum((kernel_local, bias_local), ('seq', 'dp'))]
  transfers between devices with their start and end apart: 13 -> 13, of which waited for: 11 -> 9; matrix products, arithmetic and copies ran while one was open for 18% -> 19% of each run, Pallas kernels for 0% -> 0%
where the time goes in v1:
time: 300 us; the launch traced here: 298 us
  waiting for transfers between devices  106 us (35%)
  local copies, waits for them, and re-layouts  44.2 us (15%)
  blocking collectives  40.8 us (14%)
  starting transfers between devices  38.2 us (13%)
  other arithmetic  32.5 us (11%)
  matrix products  19.2 us (6%)
  between operations  17.3 us (6%)
    reduce_scatter x1, waiting for transfers between devices, on_device(): lax.psum_scatter(term_block, 'seq', scatter_dimension=0, tiled=True)  75.6 us
    psum x1, blocking collectives, on_device(): lax.psum((kernel_local, bias_local), ('seq', 'dp'))  40.8 us
    unnamed x119, local copies, waits for them, and re-layouts  15.6 us
    reduce_sum x2, other arithmetic, on_device(): jnp.sum(grad_conv * padded[tap:tap + frames_dev], axis=0)  10.6 us
    unnamed x2, other arithmetic  7.44 us
    all_to_all x1, waiting for transfers between devices, on_device(): lax.all_to_all(value_send, 'seq', split_axis=0, concat_axis=1, tiled=True)  7.34 us
    all_to_all x1, starting transfers between devices, on_device(): lax.all_to_all(to_serving(query_local), 'seq', split_axis=0, concat_axis=...  7.28 us
    ppermute x2, starting transfers between devices, with_halo(): before = lax.ppermute(last, axis, up)  6.91 us
  transfers between devices with their start and end apart: 13, of which 9 were waited for; matrix products, arithmetic and copies ran while one was open for 19% of the time, Pallas kernels for 0%

profile of v1, /device:TPU:0, one launch (start us, length us, event | category | flops | bytes accessed | tf_op | source)
XLA Modules:
  0.0 297.8 jit_solution(16587339482942641711)
XLA Ops:
  9.9 7.3 %all-to-all-start = ((bf16[8,128,96]{1,2,0:T(8,128)(2,1)}), bf16[8,128,96]{1,2,0:T(8,128)(2,1)S(1)}, u32[]{:S(2)}, u32[]{:S(2)}) async-start(bf16[8,128,96]{1,2,0:T(8,128)(2,1)} %bitcast.3), calls=%async_computation | async-start | bytes 393216 | tf_op jit(solution)/shard_map/all_to_all | solution.py:107
  18.9 6.2 %all-to-all-done = bf16[8,128,96]{1,2,0:T(8,128)(2,1)S(1)} async-done(((bf16[8,128,96]{1,2,0:T(8,128)(2,1)}), bf16[8,128,96]{1,2,0:T(8,128)(2,1)S(1)}, u32[]{:S(2)}, u32[]{:S(2)}) %all-to-all-start) | async-done | bytes 196640 | tf_op jit(solution)/shard_map/all_to_all | solution.py:107
  25.1 3.4 %all-to-all-start.1 = ((bf16[8,128,96]{1,2,0:T(8,128)(2,1)}), bf16[8,128,96]{1,2,0:T(8,128)(2,1)S(1)}, u32[]{:S(2)}, u32[]{:S(2)}) async-start(bf16[8,128,96]{1,2,0:T(8,128)(2,1)} %bitcast.5), calls=%async_computation.1 | async-start | bytes 393216 | tf_op jit(solution)/shard_map/all_to_all | solution.py:117
  30.3 6.0 %all-to-all-done.1 = bf16[8,128,96]{1,2,0:T(8,128)(2,1)S(1)} async-done(((bf16[8,128,96]{1,2,0:T(8,128)(2,1)}), bf16[8,128,96]{1,2,0:T(8,128)(2,1)S(1)}, u32[]{:S(2)}, u32[]{:S(2)}) %all-to-all-start.1) | async-done | bytes 196640 | tf_op jit(solution)/shard_map/all_to_all | solution.py:117
  36.3 3.4 %all-to-all-start.2 = ((bf16[8,128,96]{1,2,0:T(8,128)(2,1)}), bf16[8,128,96]{1,2,0:T(8,128)(2,1)S(1)}, u32[]{:S(2)}, u32[]{:S(2)}) async-start(bf16[8,128,96]{1,2,0:T(8,128)(2,1)} %bitcast.7), calls=%async_computation.2 | async-start | bytes 393216 | tf_op jit(solution)/shard_map/all_to_all | solution.py:118
  40.0 7.3 %all-to-all-done.2 = bf16[8,128,96]{1,2,0:T(8,128)(2,1)S(1)} async-done(((bf16[8,128,96]{1,2,0:T(8,128)(2,1)}), bf16[8,128,96]{1,2,0:T(8,128)(2,1)S(1)}, u32[]{:S(2)}, u32[]{:S(2)}) %all-to-all-start.2) | async-done | bytes 196640 | tf_op jit(solution)/shard_map/all_to_all | solution.py:118
  47.6 4.6 %while.24 = (s32[]{:T(128)}, bf16[2,512,96]{1,2,0:T(8,128)(2,1)S(1)}, f32[2,512]{1,0:T(2,128)S(1)}, bf16[2,512,96]{2,1,0:T(8,128)(2,1)S(1)}, bf16[1024,96]{1,0:T...) while((s32[]{:T(128)}, ...), condition=%wide.region_3.4_spmd.clone, body=%wide.region_0.3_spmd.clone.sunk | while | flops 204997120 | bytes 7164021 | solution.py:45
  56.3 3.7 %reduce.64 = bf16[1024,96]{1,0:T(8,128)(2,1)} reduce(bf16[1024,1,96]{2,1,0:T(2,128)(2,1)} %bitcast.116, bf16[]{:T(256)} %broadcast.73), dimensions={1}, to_apply=%bitcast.67.reduce_sub_computation | reduce | bytes 393218
  62.1 3.4 %all-to-all-start.3 = ((bf16[8,2,6144]{2,1,0:T(2,128)(2,1)}), bf16[8,2,6144]{2,1,0:T(2,128)(2,1)S(1)}, u32[]{:S(2)}, u32[]{:S(2)}) async-start(bf16[8,2,6144]{2,1,0:T(2,128)(2,1)} %reshape.156), calls=%async_computation.3 | async-start | bytes 393216 | tf_op jit(solution)/shard_map/all_to_all | solution.py:125
  69.3 4.0 %all-to-all-done.3 = bf16[8,2,6144]{2,1,0:T(2,128)(2,1)S(1)} async-done(((bf16[8,2,6144]{2,1,0:T(2,128)(2,1)}), bf16[8,2,6144]{2,1,0:T(2,128)(2,1)S(1)}, u32[]{:S(2)}, u32[]{:S(2)}) %all-to-all-start.3) | async-done | bytes 196640 | tf_op jit(solution)/shard_map/all_to_all | solution.py:125
  83.5 3.0 %collective-permute-done.1 = bf16[15,1536]{1,0:T(8,128)(2,1)S(1)} collective-permute-done((bf16[15,1536]{1,0:T(8,128)(2,1)S(1)}, bf16[15,1536]{1,0:T(8,128)(2,1)S(1)}, u32[]{:S(2)}, u32[]{:S(2)}) %collective-permute-start.1) | collective-permute-done | bytes 46112 | tf_op jit(solution)/shard_map/ppermute | solution.py:22
  86.9 7.5 %multiply_reduce_fusion = (f32[1536]{0:T(1024)}, f32[1536]{0:T(1024)}, f32[1536]{0:T(1024)}, f32[1536]{0:T(1024)}, f32[1536]{0:T(1024)}, /*index=5*/f32[1536]{0:...) fusion(f32[158,1536]{1,0:T(8,128)S(1)} %maximum_convert_fusion,, ...), kind=kLoop, calls=%fused_computation.190 | loop fusion | flops 21206016 | bytes 26652800 | tf_op jit(solution)/shard_map/reduce_sum | solution.py:143
  95.7 5.0 %collective-permute-start.3 = (f32[15,1536]{1,0:T(8,128)S(1)}, f32[15,1536]{1,0:T(8,128)S(1)}, u32[]{:S(2)}, u32[]{:S(2)}) collective-permute-start(f32[15,1536]{1,0:T(8,128)S(1)} %get-tuple-element.306), channel_id=1, source_target_pairs={{0,4},{4,8},{8,12},{12,16},{16,20},{20,24},{24,28},{1,5},{5,9},{9,... | collective-permute-start | bytes 276488 | tf_op jit(solution)/shard_map/ppermute | solution.py:21
  102.7 3.7 %fusion.37 = bf16[128,1536]{1,0:T(8,128)(2,1)S(1)} fusion(f32[128,1536]{1,0:T(8,128)S(1)} %get-tuple-element.299, f32[15,1536]{1,0:T(8,128)S(1)} %collective-permute-done.3, f32[15,1536]{1,0:T(8,128)S(1)} %collective-permute-done.2, bf16[1,128,1536]{2,1,0:T(8,128)(2,1)S(1)} %copy-done.11, f32[1536]{0:T(1024)S(1)} %get-tuple-element.265, ...), kind=kLoop, calls=%fused_computation.100 | loop fusion | flops 18874368 | bytes 1947776 | tf_op jit(solution)/shard_map/convert_element_type | solution.py:151
  115.5 6.7 %all-to-all-start.4 = ((bf16[8,128,96]{1,2,0:T(8,128)(2,1)}), bf16[8,128,96]{1,2,0:T(8,128)(2,1)S(1)}, u32[]{:S(2)}, u32[]{:S(2)}) async-start(bf16[8,128,96]{1,2,0:T(8,128)(2,1)} %bitcast.123), calls=%async_computation.4 | async-start | bytes 393216 | tf_op jit(solution)/shard_map/all_to_all | solution.py:157
  122.4 3.0 %multiply_reduce_fusion.18 = (f32[1536]{0:T(1024)S(1)}, f32[1536]{0:T(1024)S(1)}, f32[1536]{0:T(1024)S(1)}, f32[1536]{0:T(1024)S(1)}, f32[1536]{0:T(1024)S(1)}, ...) fusion(f32[128,1536]{1,0:T(8,128)} %copy-done.7, ...), kind=kLoop, calls=%fused_computation.208 | loop fusion | flops 5286912 | bytes 11096064 | tf_op jit(solution)/shard_map/reduce_sum | solution.py:143
  128.9 3.5 %stack.127 = f32[31,1536]{1,0:T(8,128)} concatenate(f32[1,1536]{1,0:T(1,128)} %stack.96, f32[1,1536]{1,0:T(1,128)} %stack.97, f32[1,1536]{1,0:T(1,128)} %stack.98, f32[1,1536]{1,0:T(1,128)} %stack.99, f32[1,1536]{1,0:T(1,128)} %stack.100, f32[1,1536]{1,0:T(1,128)S(1)} %stack.101, f32[1,1536]{1,0:T(1,128)S(1)} %stack.102, f32[1,1536]{1,0:T(1,128)S(1)} %stack.103, ...), dimensions={0} | concatenate | bytes 380928 | tf_op jit(solution)/shard_map/stack | solution.py:142
  135.9 75.6 %reduce-scatter.2.cloned.1.call-done = f32[192,768]{1,0:T(8,128)} async-done(((f32[1536,768]{1,0:T(8,128)}), f32[192,768]{1,0:T(8,128)}) %reduce-scatter.2.cloned.1.call-update) | async-done | bytes 589840 | tf_op jit(solution)/shard_map/reduce_scatter | solution.py:170
  214.0 12.8 %while.25 = (s32[]{:T(128)}, bf16[2,512,96]{1,2,0:T(8,128)(2,1)}, bf16[2,512,96]{2,1,0:T(8,128)(2,1)S(1)}, bf16[1024,96]{1,0:T(8,128)(2,1)S(1)}, f32[2,512]{1,0:...) while((s32[]{:T(128)}, bf16[2,512,96]{1,2,0:T(8,128)(2,1)}, ...), condition=%wide.region_6.7_spmd.clone, body=%wide.region_5.6_spmd.clone.sunk | while | flops 305185792 | bytes 6241429 | solution.py:73
  217.2 3.2 %fusion.163 = bf16[2,512,96]{1,2,0:T(8,128)(2,1)} fusion(bf16[2,512,96]{1,2,0:T(8,128)(2,1)} %get-tuple-element.455, s32[]{:T(128)S(6)} %copy.133, bf16[1024,96]{1,0:T(8,128)(2,1)S(1)} %get-tuple-element.467, f32[512,1024]{1,0:T(8,128)} %fusion.162, bf16[1024,96]{1,0:T(8,128)(2,1)S(1)} %get-tuple-element.470, f32[512]{0:T(512)S(1)} %bitcast.131, ...), kind=kOutput, calls=%fused_computation.17.clone.1 | convolution fusion | flops 204521472 | bytes 2955264 | tf_op jit(solution)/shard_map/while/body/eval_jaxpr/dot_general | solution.py:71
  223.6 3.2 %fusion.163 = bf16[2,512,96]{1,2,0:T(8,128)(2,1)} fusion(bf16[2,512,96]{1,2,0:T(8,128)(2,1)} %get-tuple-element.455, s32[]{:T(128)S(6)} %copy.133, bf16[1024,96]{1,0:T(8,128)(2,1)S(1)} %get-tuple-element.467, f32[512,1024]{1,0:T(8,128)} %fusion.162, bf16[1024,96]{1,0:T(8,128)(2,1)S(1)} %get-tuple-element.470, f32[512]{0:T(512)S(1)} %bitcast.131, ...), kind=kOutput, calls=%fused_computation.17.clone.1 | convolution fusion | flops 204521472 | bytes 2955264 | tf_op jit(solution)/shard_map/while/body/eval_jaxpr/dot_general | solution.py:71
  231.2 3.7 %reduce.65 = bf16[1024,96]{1,0:T(8,128)(2,1)} reduce(bf16[1024,1,96]{2,1,0:T(2,128)(2,1)} %bitcast.117, bf16[]{:T(256)} %broadcast.73), dimensions={1}, to_apply=%bitcast.69.reduce_sub_computation | reduce | bytes 393218
  237.0 4.5 %all-to-all-start.5 = ((bf16[8,2,6144]{2,1,0:T(2,128)(2,1)}), bf16[8,2,6144]{2,1,0:T(2,128)(2,1)}, u32[]{:S(2)}, u32[]{:S(2)}) async-start(bf16[8,2,6144]{2,1,0:T(2,128)(2,1)} %reshape.158), calls=%async_computation.5 | async-start | bytes 393216 | tf_op jit(solution)/shard_map/all_to_all | solution.py:165
  242.6 40.8 %psum.15 = f32[1536]{0:T(1024)S(1)} all-reduce(f32[1536]{0:T(1024)S(1)} %copy-done.48), channel_id=1, replica_groups=mesh['seq'=8,'dp'=4] {'seq','dp'}, use_global_device_ids=true, to_apply=%region_42.43 | all-reduce | flops 1536 | bytes 12288 | tf_op jit(solution)/shard_map/psum | solution.py:172
  (219 shorter events, 72.5 us)
Async XLA Ops:
  8.0 67.6 %copy-start = (bf16[1536,768]{1,0:T(8,128)(2,1)S(1)}, bf16[1536,768]{1,0:T(8,128)(2,1)}, u32[]{:S(2)}) copy-start(bf16[1536,768]{1,0:T(8,128)(2,1)} %param.18) | copy-start | bytes 7077892
  9.9 15.2 %all-to-all-start = ((bf16[8,128,96]{1,2,0:T(8,128)(2,1)}), bf16[8,128,96]{1,2,0:T(8,128)(2,1)S(1)}, u32[]{:S(2)}, u32[]{:S(2)}) async-start(bf16[8,128,96]{1,2,0:T(8,128)(2,1)} %bitcast.3), calls=%async_computation | async-start | bytes 393216 | tf_op jit(solution)/shard_map/all_to_all | solution.py:107
  25.1 11.1 %all-to-all-start.1 = ((bf16[8,128,96]{1,2,0:T(8,128)(2,1)}), bf16[8,128,96]{1,2,0:T(8,128)(2,1)S(1)}, u32[]{:S(2)}, u32[]{:S(2)}) async-start(bf16[8,128,96]{1,2,0:T(8,128)(2,1)} %bitcast.5), calls=%async_computation.1 | async-start | bytes 393216 | tf_op jit(solution)/shard_map/all_to_all | solution.py:117
  36.3 11.1 %all-to-all-start.2 = ((bf16[8,128,96]{1,2,0:T(8,128)(2,1)}), bf16[8,128,96]{1,2,0:T(8,128)(2,1)S(1)}, u32[]{:S(2)}, u32[]{:S(2)}) async-start(bf16[8,128,96]{1,2,0:T(8,128)(2,1)} %bitcast.7), calls=%async_computation.2 | async-start | bytes 393216 | tf_op jit(solution)/shard_map/all_to_all | solution.py:118
  52.2 14.0 %copy-start.49 = (f32[2,512]{1,0:T(2,128)}, f32[2,512]{1,0:T(2,128)S(1)}, u32[]{:S(2)}) copy-start(f32[2,512]{1,0:T(2,128)S(1)} %get-tuple-element.448) | copy-start | bytes 12292
  52.3 23.3 %copy-start.1 = (bf16[1024,96]{1,0:T(8,128)(2,1)}, bf16[1024,96]{1,0:T(8,128)(2,1)S(1)}, u32[]{:S(2)}) copy-start(bf16[1024,96]{1,0:T(8,128)(2,1)S(1)} %get-tuple-element.477) | copy-start | bytes 589828
  52.3 23.3 %copy-start.3 = (bf16[1024,96]{1,0:T(8,128)(2,1)}, bf16[1024,96]{1,0:T(8,128)(2,1)S(1)}, u32[]{:S(2)}) copy-start(bf16[1024,96]{1,0:T(8,128)(2,1)S(1)} %get-tuple-element.480) | copy-start | bytes 589828
  52.3 23.3 %copy-start.5 = (bf16[2,512,96]{2,1,0:T(8,128)(2,1)}, bf16[2,512,96]{2,1,0:T(8,128)(2,1)S(1)}, u32[]{:S(2)}) copy-start(bf16[2,512,96]{2,1,0:T(8,128)(2,1)S(1)} %get-tuple-element.481) | copy-start | bytes 589828
  62.1 11.1 %all-to-all-start.3 = ((bf16[8,2,6144]{2,1,0:T(2,128)(2,1)}), bf16[8,2,6144]{2,1,0:T(2,128)(2,1)S(1)}, u32[]{:S(2)}, u32[]{:S(2)}) async-start(bf16[8,2,6144]{2,1,0:T(2,128)(2,1)} %reshape.156), calls=%async_computation.3 | async-start | bytes 393216 | tf_op jit(solution)/shard_map/all_to_all | solution.py:125
  65.5 145.9 %reduce-scatter.2.cloned.1.call-start = ((), (), s32[]{:S(2)}) async-start(), calls=%async_computation.7 | async-start | bytes 5308416 | tf_op jit(solution)/shard_map/reduce_scatter | solution.py:170
  78.6 4.9 %collective-permute-start = (bf16[15,1536]{1,0:T(8,128)(2,1)S(1)}, bf16[15,1536]{1,0:T(8,128)(2,1)S(1)}, u32[]{:S(2)}, u32[]{:S(2)}) collective-permute-start(bf16[15,1536]{1,0:T(8,128)(2,1)S(1)} %get-tuple-element.307), channel_id=1, source_target_pairs={{0,4},{4,8},{8,12},{12,16},{16,20},{20,24},{24,28},{1,5},{5,9},{9,... | collective-permute-start | bytes 138248 | tf_op jit(solution)/shard_map/ppermute | solution.py:21
  80.6 6.0 %collective-permute-start.1 = (bf16[15,1536]{1,0:T(8,128)(2,1)S(1)}, bf16[15,1536]{1,0:T(8,128)(2,1)S(1)}, u32[]{:S(2)}, u32[]{:S(2)}) collective-permute-start(bf16[15,1536]{1,0:T(8,128)(2,1)S(1)} %get-tuple-element.308), channel_id=1, source_target_pairs={{4,0},{8,4},{12,8},{16,12},{20,16},{24,20},{28,24},{5,1},{9,5},{13... | collective-permute-start | bytes 138248 | tf_op jit(solution)/shard_map/ppermute | solution.py:22
  94.4 6.7 %collective-permute-start.2 = (f32[15,1536]{1,0:T(8,128)S(1)}, f32[15,1536]{1,0:T(8,128)S(1)}, u32[]{:S(2)}, u32[]{:S(2)}) collective-permute-start(f32[15,1536]{1,0:T(8,128)S(1)} %get-tuple-element.305), channel_id=1, source_target_pairs={{4,0},{8,4},{12,8},{16,12},{20,16},{24,20},{28,24},{5,1},{9,5},{13... | collective-permute-start | bytes 276488 | tf_op jit(solution)/shard_map/ppermute | solution.py:22
  95.7 7.0 %collective-permute-start.3 = (f32[15,1536]{1,0:T(8,128)S(1)}, f32[15,1536]{1,0:T(8,128)S(1)}, u32[]{:S(2)}, u32[]{:S(2)}) collective-permute-start(f32[15,1536]{1,0:T(8,128)S(1)} %get-tuple-element.306), channel_id=1, source_target_pairs={{0,4},{4,8},{8,12},{12,16},{16,20},{20,24},{24,28},{1,5},{5,9},{9,... | collective-permute-start | bytes 276488 | tf_op jit(solution)/shard_map/ppermute | solution.py:21
  115.5 18.4 %all-to-all-start.4 = ((bf16[8,128,96]{1,2,0:T(8,128)(2,1)}), bf16[8,128,96]{1,2,0:T(8,128)(2,1)S(1)}, u32[]{:S(2)}, u32[]{:S(2)}) async-start(bf16[8,128,96]{1,2,0:T(8,128)(2,1)} %bitcast.123), calls=%async_computation.4 | async-start | bytes 393216 | tf_op jit(solution)/shard_map/all_to_all | solution.py:157
  122.2 161.8 %all-reduce.2.cloned.1.call-start = ((), (), s32[]{:S(2)}) async-start(), calls=%async_computation.8 | async-start | bytes 393216 | tf_op jit(solution)/shard_map/psum | solution.py:172
  125.4 88.6 %copy-start.2 = (bf16[1024,96]{1,0:T(8,128)(2,1)S(1)}, bf16[1024,96]{1,0:T(8,128)(2,1)}, u32[]{:S(2)}) copy-start(bf16[1024,96]{1,0:T(8,128)(2,1)} %copy-done.1) | copy-start | bytes 589828
  125.4 88.6 %copy-start.4 = (bf16[1024,96]{1,0:T(8,128)(2,1)S(1)}, bf16[1024,96]{1,0:T(8,128)(2,1)}, u32[]{:S(2)}) copy-start(bf16[1024,96]{1,0:T(8,128)(2,1)} %copy-done.3) | copy-start | bytes 589828
  125.4 88.6 %copy-start.6 = (bf16[2,512,96]{2,1,0:T(8,128)(2,1)S(1)}, bf16[2,512,96]{2,1,0:T(8,128)(2,1)}, u32[]{:S(2)}) copy-start(bf16[2,512,96]{2,1,0:T(8,128)(2,1)} %copy-done.5) | copy-start | bytes 589828
  132.4 155.6 %all-gather.3.cloned.1.call-start = ((), (), s32[]{:S(2)}) async-start(), calls=%async_computation.9 | async-start | bytes 1474560 | tf_op jit(solution)/shard_map/all_gather | solution.py:171
  226.7 14.8 %copy-start.9 = (f32[128,1536]{1,0:T(8,128)S(1)}, f32[128,1536]{1,0:T(8,128)}, u32[]{:S(2)}) copy-start(f32[128,1536]{1,0:T(8,128)} %get-tuple-element.300) | copy-start | bytes 2359300
  226.7 14.8 %copy-start.10 = (bf16[128,1536]{1,0:T(8,128)(2,1)S(1)}, bf16[128,1536]{1,0:T(8,128)(2,1)}, u32[]{:S(2)}) copy-start(bf16[128,1536]{1,0:T(8,128)(2,1)} %get-tuple-element.310) | copy-start | bytes 1179652
  226.8 14.8 %copy-start.51 = (pred[128]{0:T(512)(128)(4,1)S(1)}, pred[128]{0:T(512)(128)(4,1)}, u32[]{:S(2)}) copy-start(pred[128]{0:T(512)(128)(4,1)} %add_compare_fusion) | copy-start | bytes 388
  237.0 48.5 %all-to-all-start.5 = ((bf16[8,2,6144]{2,1,0:T(2,128)(2,1)}), bf16[8,2,6144]{2,1,0:T(2,128)(2,1)}, u32[]{:S(2)}, u32[]{:S(2)}) async-start(bf16[8,2,6144]{2,1,0:T(2,128)(2,1)} %reshape.158), calls=%async_computation.5 | async-start | bytes 393216 | tf_op jit(solution)/shard_map/all_to_all | solution.py:165
  (43 other events, 310.1 us)
Sparse Core Ops, SparseCore 0:
  110.3 101.0 reduce-scatter.1
  213.4 17.3 all-gather.2
Sparse Core Ops, SparseCore 1:
  132.5 142.2 all-reduce.1
